TPU v7x, 512 devices: a whole 4x4x16 slice. The times are simulated.
512 devices in a mesh: sec: 2 (over z_hi), gx: 16 (over z_lo, core), gy: 16 (over x, y).
Axes of the slice: x: 4, y: 4, z: 16 (z_hi: 2, z_lo: 8; z = z_hi * 8 + z_lo), core: 2. Of those that a mesh axis runs over, the one named last changes fastest.
Arguments:
- terminal: float32 [4, 16, 256, 4096], P('sec', None, 'gx', 'gy'), may hold values from -6 to 6
- forward_temp: bfloat16 [2, 4, 16, 256, 4096], P(None, 'sec', None, 'gx', 'gy'), may hold values from -6 to 6
- conductivity: float32 [16, 256, 4096], P(None, 'gx', 'gy'), may hold values from 0.02 to 0.15
- velocity: float32 [2, 16, 256, 4096], P(None, None, 'gx', 'gy'), may hold values from -0.3 to 0.3
- fixed_mask: int32 [16, 256, 4096], P(None, 'gx', 'gy'), may hold values 0 or 1
- wells: int32 [4, 8, 3], P('sec'), may hold values from 0 to 4095, as said below
- misfit: float32 [2, 4, 8], P(None, 'sec'), may hold values from -12 to 12
- head_gradient: bfloat16 [2, 16, 256, 4096], P('sec', None, 'gx', 'gy'), may hold values from -6 to 6
- blocks: bfloat16 [32, 7, 128, 128], P('gy'), may hold values from -0.1875 to 0.1875
- block_cols: int32 [32, 7], P('gy'), may hold values from 0 to 31, as said below
Outputs:
- head_adjoint: float32 [2, 16, 256, 4096], P('sec', None, 'gx', 'gy')
- sensitivity: float32 [16, 256, 4096], P(None, 'gx', 'gy')
Inputs may be any that keep to these rules, and one draw needn't show every extreme that they name: `wells`: each row is one cell (z, x, y) with z < 16, x < 256, y < 4096; the first test observes the cells (0, 0, 0) and (15, 255, 4095). `block_cols`: row r lists 7 different block columns, the first of which is r.
All inputs are finite; a program needn't handle non-finite values. No bound on the sum of `fixed_mask` on one device may be relied on, other than what follows from the above.
Results may differ from a plain program's by a relative error of at most 0.0029.
Values may be sent and summed in bfloat16 or wider, within the bound.
No kernel may reach another device: no remote copies, remote signals or barrier semaphores. Data moves between devices by JAX's collectives and lax.ppermute only.
A program may use at most 64 MiB of HBM per device.

v0:
```python
import jax
import jax.numpy as jnp
from jax import lax
from jax.sharding import PartitionSpec as P


def extended(cells, sides, width):
    for axis, dim in sides:
        count = lax.axis_size(axis)
        ends = count - 1
        head = lax.slice_in_dim(cells, 0, width, axis=dim)
        tail = lax.slice_in_dim(cells, cells.shape[dim] - width, cells.shape[dim], axis=dim)
        cells = jnp.concatenate(
            [
                lax.ppermute(tail, axis, [(i, (i + 1) % count) for i in range(ends)]),
                cells,
                lax.ppermute(head, axis, [((i + 1) % count, i) for i in range(ends)]),
            ],
            axis=dim,
        )
    return cells


def shifted(padded):
    lead = [(0, 0)] * (padded.ndim - 3)
    deeper = jnp.pad(padded, lead + [(1, 1), (0, 0), (0, 0)])
    centre = deeper[..., 1:-1, 1:-1, 1:-1]
    beside_all = [
        deeper[..., 2:, 1:-1, 1:-1],
        deeper[..., :-2, 1:-1, 1:-1],
        deeper[..., 1:-1, 2:, 1:-1],
        deeper[..., 1:-1, :-2, 1:-1],
        deeper[..., 1:-1, 1:-1, 2:],
        deeper[..., 1:-1, 1:-1, :-2],
    ]
    return (centre, beside_all)


def face_weights(kappa_pad):
    centre, beside_all = shifted(kappa_pad)
    return [
        2.0 * centre * other / jnp.where(centre + other > 0.0, centre + other, 1.0)
        for other in beside_all
    ]


def advance(adjoint_pad, weights, keep, speed_x, speed_y, source):
    centre, beside_all = shifted(adjoint_pad)
    diffusion = weights[0] * (beside_all[0] - centre)
    for face in range(1, 6):
        diffusion = diffusion + weights[face] * (beside_all[face] - centre)
    slope_x = 0.5 * (beside_all[2] - beside_all[3])
    slope_y = 0.5 * (beside_all[4] - beside_all[5])
    updated = keep * (centre + diffusion + speed_x * slope_x + speed_y * slope_y + source)
    return (updated, diffusion, slope_x, slope_y)


def well_sources(wells, misfit_level, layers, rows_x, cols_y, margin):
    start_x = lax.axis_index("gx") * rows_x - margin
    start_y = lax.axis_index("gy") * cols_y - margin
    coord_z = jnp.arange(layers, dtype=jnp.int32)[:, None, None]
    coord_x = (start_x + jnp.arange(rows_x + 2 * margin, dtype=jnp.int32))[None, :, None]
    coord_y = (start_y + jnp.arange(cols_y + 2 * margin, dtype=jnp.int32))[None, None, :]
    well_z = wells[:, :, 0][:, :, None, None, None]
    well_x = wells[:, :, 1][:, :, None, None, None]
    well_y = wells[:, :, 2][:, :, None, None, None]
    matches = (coord_z == well_z) & (coord_x == well_x) & (coord_y == well_y)
    return jnp.sum(jnp.where(matches, misfit_level[:, :, None, None, None], 0.0), axis=1)


def shards(
    terminal,
    forward_temp,
    conductivity,
    velocity,
    fixed_mask,
    wells,
    misfit,
    head_gradient,
    blocks,
    block_cols,
):
    layers, rows_x, cols_y = conductivity.shape
    steps = forward_temp.shape[0]
    keep = 1.0 - fixed_mask.astype(jnp.float32)
    heat_sens = jnp.zeros((layers, rows_x, cols_y), jnp.float32)
    flow_x = jnp.zeros((layers, rows_x, cols_y), jnp.float32)
    flow_y = jnp.zeros((layers, rows_x, cols_y), jnp.float32)
    kappa_pad = extended(conductivity, (("gx", 1), ("gy", 2)), 1)
    weights = face_weights(kappa_pad)
    adjoint = terminal
    for level in reversed(range(steps)):
        padded = extended(adjoint, (("gx", 2), ("gy", 3)), 1)
        source = well_sources(wells, misfit[level], layers, rows_x, cols_y, 0)
        adjoint, diffusion, slope_x, slope_y = advance(
            padded, weights, keep, velocity[0], velocity[1], source
        )
        temper = forward_temp[level].astype(jnp.float32)
        heat_sens = heat_sens + jnp.sum(temper * diffusion, axis=0)
        flow_x = flow_x + jnp.sum(temper * slope_x, axis=0)
        flow_y = flow_y + jnp.sum(temper * slope_y, axis=0)
    first = lax.axis_index("sec") == 0
    mine = jnp.where(first, flow_x, flow_y)
    other = jnp.where(first, flow_y, flow_x)
    partner = [(0, 1), (1, 0)]
    rounded = (mine + lax.ppermute(other, "sec", partner)).astype(jnp.bfloat16)
    row_blocks, per_row, block_size, _ = blocks.shape
    piece = lax.all_gather(rounded, "gy", axis=2, tiled=True)
    count = piece.shape[2] // block_size
    split_rows = piece.reshape(layers, rows_x, count, block_size)
    block_ids = jnp.arange(count, dtype=jnp.int32)
    chosen = (block_cols[:, :, None] == block_ids[None, None, :]).astype(jnp.bfloat16)
    portion = jnp.einsum("bkq,zxqj->bkzxj", chosen, split_rows, preferred_element_type=jnp.float32)
    picked = portion.astype(jnp.bfloat16)
    head = jnp.einsum(
        "bkzxj,bkij->zxbi", picked, blocks, preferred_element_type=jnp.float32
    ).reshape(layers, rows_x, cols_y)
    partial_sens = heat_sens + head * head_gradient[0].astype(jnp.float32)
    sensitivity = partial_sens + lax.ppermute(partial_sens, "sec", partner)
    return (head[None], sensitivity)


def solution(mesh):
    placed = (
        P("sec", None, "gx", "gy"),
        P(None, "sec", None, "gx", "gy"),
        P(None, "gx", "gy"),
        P(None, None, "gx", "gy"),
        P(None, "gx", "gy"),
        P("sec", None, None),
        P(None, "sec", None),
        P("sec", None, "gx", "gy"),
        P("gy", None, None, None),
        P("gy", None),
    )
    return jax.shard_map(
        shards,
        mesh=mesh,
        in_specs=placed,
        out_specs=(P("sec", None, "gx", "gy"), P(None, "gx", "gy")),
        check_vma=False,
    )
```

profile of v0, /device:TPU:32, one launch (start us, length us, event | category | flops | bytes accessed | tf_op | source)
XLA Modules:
  0.0 226.1 jit_solution(11138354482306704369)
XLA Ops:
  7.2 0.0 all-gather.2.cloned.1.call-start
  7.3 1.1 fusion.57
  8.3 1.9 collective-permute-start.2
  10.2 3.6 %collective-permute-start.3 = (f32[16,1,256]{2,1,0:T(1,128)S(1)}, f32[16,1,256]{2,1,0:T(1,128)S(1)}, u32[]{:S(2)}, u32[]{:S(2)}) collective-permute-start(f32[16,1,256]{2,1,0:T(1,128)S(1)} %get-tuple-element.30), channel_id=1, source_target_pairs={{16,0},{32,16},{48,32},{64,48},{80,64},{96,80},{112,96},{128,112},... | collective-permute-start | bytes 49160 | tf_op jit(solution)/shard_map/ppermute | solution.py:17
  13.9 1.1 fusion.55
  15.0 5.1 %collective-permute-start = (f32[2,16,1,256]{3,2,1,0:T(1,128)S(1)}, f32[2,16,1,256]{3,2,1,0:T(1,128)S(1)}, u32[]{:S(2)}, u32[]{:S(2)}) collective-permute-start(f32[2,16,1,256]{3,2,1,0:T(1,128)S(1)} %get-tuple-element.19), channel_id=1, source_target_pairs={{16,0},{32,16},{48,32},{64,48},{80,64},{96,80},{112,96},{128,112},... | collective-permute-start | bytes 98312 | tf_op jit(solution)/shard_map/ppermute | solution.py:17
  20.1 1.9 collective-permute-start.1
  22.1 0.7 slice_bitcast_fusion.3
  22.8 1.1 multiply_bitcast_fusion.1
  23.9 0.1 iota_compare_fusion.4
  24.0 0.1 broadcast_and_fusion
  24.1 0.1 broadcast_compare_fusion
  24.2 0.1 pad_maximum_fusion.18
  24.3 0.1 fusion.56
  24.4 1.4 collective-permute-start.4
  25.8 1.3 collective-permute-start.5
  27.1 0.8 select_reduce_fusion
  28.0 3.1 %collective-permute-done.4 = f32[16,18,1]{2,1,0:T(8,128)S(1)} collective-permute-done((f32[16,18,1]{2,1,0:T(8,128)S(1)}, f32[16,18,1]{2,1,0:T(8,128)S(1)}, u32[]{:S(2)}, u32[]{:S(2)}) %collective-permute-start.4) | collective-permute-done | bytes 1184 | tf_op jit(solution)/shard_map/ppermute | solution.py:15
  31.1 4.2 %collective-permute-done.5 = f32[16,18,1]{2,1,0:T(8,128)S(1)} collective-permute-done((f32[16,18,1]{2,1,0:T(8,128)S(1)}, f32[16,18,1]{2,1,0:T(8,128)S(1)}, u32[]{:S(2)}, u32[]{:S(2)}) %collective-permute-start.5) | collective-permute-done | bytes 1184 | tf_op jit(solution)/shard_map/ppermute | solution.py:17
  35.2 0.4 select_maximum_fusion.8
  35.7 0.1 pad_maximum_fusion
  35.8 0.2 fusion.53
  36.0 2.9 %collective-permute-start.6 = (f32[2,16,18,1]{3,2,1,0:T(8,128)S(1)}, f32[2,16,18,1]{3,2,1,0:T(8,128)S(1)}, u32[]{:S(2)}, u32[]{:S(2)}) collective-permute-start(f32[2,16,18,1]{3,2,1,0:T(8,128)S(1)} %get-tuple-element.14), channel_id=1, source_target_pairs={{0,1},{1,2},{2,3},{3,4},{4,5},{5,6},{6,7},{7,8},{8,9},{9,10},{10,1... | collective-permute-start | bytes 6920 | tf_op jit(solution)/shard_map/ppermute | solution.py:15
  38.9 1.3 collective-permute-start.7
  40.2 0.6 fusion.41
  40.8 6.7 %collective-permute-done.6 = f32[2,16,18,1]{3,2,1,0:T(8,128)S(1)} collective-permute-done((f32[2,16,18,1]{3,2,1,0:T(8,128)S(1)}, f32[2,16,18,1]{3,2,1,0:T(8,128)S(1)}, u32[]{:S(2)}, u32[]{:S(2)}) %collective-permute-start.6) | collective-permute-done | bytes 2336 | tf_op jit(solution)/shard_map/ppermute | solution.py:15
  47.5 4.1 %collective-permute-done.7 = f32[2,16,18,1]{3,2,1,0:T(8,128)S(1)} collective-permute-done((f32[2,16,18,1]{3,2,1,0:T(8,128)S(1)}, f32[2,16,18,1]{3,2,1,0:T(8,128)S(1)}, u32[]{:S(2)}, u32[]{:S(2)}) %collective-permute-start.7) | collective-permute-done | bytes 2336 | tf_op jit(solution)/shard_map/ppermute | solution.py:17
  51.6 0.7 select_maximum_fusion.4
  52.4 1.8 add_multiply_fusion
  54.3 1.9 collective-permute-start.8
  56.2 2.4 %collective-permute-start.9 = (f32[2,16,1,256]{3,2,1,0:T(1,128)S(1)}, f32[2,16,1,256]{3,2,1,0:T(1,128)S(1)}, u32[]{:S(2)}, u32[]{:S(2)}) collective-permute-start(f32[2,16,1,256]{3,2,1,0:T(1,128)S(1)} %get-tuple-element.16), channel_id=1, source_target_pairs={{0,16},{16,32},{32,48},{48,64},{64,80},{80,96},{96,112},{112,128},... | collective-permute-start | bytes 98312 | tf_op jit(solution)/shard_map/ppermute | solution.py:15
  58.7 2.8 %collective-permute-done.9 = f32[2,16,1,256]{3,2,1,0:T(1,128)S(1)} collective-permute-done((f32[2,16,1,256]{3,2,1,0:T(1,128)S(1)}, f32[2,16,1,256]{3,2,1,0:T(1,128)S(1)}, u32[]{:S(2)}, u32[]{:S(2)}) %collective-permute-start.9) | collective-permute-done | bytes 32800 | tf_op jit(solution)/shard_map/ppermute | solution.py:15
  61.5 0.1 pad_maximum_fusion.1
  61.6 0.2 fusion.52
  61.8 1.4 collective-permute-start.10
  63.2 5.3 %collective-permute-start.11 = (f32[2,16,18,1]{3,2,1,0:T(8,128)S(1)}, f32[2,16,18,1]{3,2,1,0:T(8,128)S(1)}, u32[]{:S(2)}, u32[]{:S(2)}) collective-permute-start(f32[2,16,18,1]{3,2,1,0:T(8,128)S(1)} %get-tuple-element.12), channel_id=1, source_target_pairs={{0,1},{1,2},{2,3},{3,4},{4,5},{5,6},{6,7},{7,8},{8,9},{9,10},{10,1... | collective-permute-start | bytes 6920 | tf_op jit(solution)/shard_map/ppermute | solution.py:15
  68.6 0.6 fusion.4
  69.1 6.4 %collective-permute-done.10 = f32[2,16,18,1]{3,2,1,0:T(8,128)S(1)} collective-permute-done((f32[2,16,18,1]{3,2,1,0:T(8,128)S(1)}, f32[2,16,18,1]{3,2,1,0:T(8,128)S(1)}, u32[]{:S(2)}, u32[]{:S(2)}) %collective-permute-start.10) | collective-permute-done | bytes 2336 | tf_op jit(solution)/shard_map/ppermute | solution.py:17
  75.6 1.2 collective-permute-done.11
  76.8 1.3 fusion.7
  78.1 0.1 broadcast_select_fusion
  78.2 13.0 %collective-permute-start.12 = (f32[16,16,256]{2,1,0:T(8,128)S(1)}, f32[16,16,256]{2,1,0:T(8,128)S(1)}, u32[]{:S(2)}, u32[]{:S(2)}) collective-permute-start(f32[16,16,256]{2,1,0:T(8,128)S(1)} %broadcast_select_fusion), channel_id=1, source_target_pairs={{0,256},{256,0},{1,257},{257,1},{2,258},{258,2},{3,259},{259,3},{4... | collective-permute-start | bytes 786440 | tf_op jit(solution)/shard_map/ppermute | solution.py:106
  91.2 10.4 %collective-permute-done.12 = f32[16,16,256]{2,1,0:T(8,128)S(1)} collective-permute-done((f32[16,16,256]{2,1,0:T(8,128)S(1)}, f32[16,16,256]{2,1,0:T(8,128)S(1)}, u32[]{:S(2)}, u32[]{:S(2)}) %collective-permute-start.12) | collective-permute-done | bytes 262176 | tf_op jit(solution)/shard_map/ppermute | solution.py:106
  101.6 0.8 add_convert_fusion
  102.4 0.7 select_maximum_fusion
  103.1 0.2 copy-done.4
  103.3 0.1 copy-done.6
  103.4 0.1 copy-done.8
  103.5 0.1 copy-done.10
  103.5 0.1 copy-done.12
  103.6 0.2 copy-done.14
  103.8 1.7 fusion.9
  105.5 76.5 %all-gather.2.cloned.1.call-done = bf16[16,16,4096]{2,1,0:T(8,128)(2,1)} async-done(((bf16[16,16,256]{2,1,0:T(8,128)(2,1)}), bf16[16,16,4096]{2,1,0:T(8,128)(2,1)}) %all-gather.2.cloned.1.call-update) | async-done | bytes 2097168 | tf_op jit(solution)/shard_map/all_gather | solution.py:108
  181.9 2.1 copy.21
  184.0 0.5 convolution_convert_fusion
  184.6 0.4 fusion.1
  185.0 0.5 copy-done.16
  185.5 0.1 copy-done.17
  185.6 0.1 fusion.43
  185.7 11.9 %collective-permute-start.13 = (f32[16,16,256]{2,1,0:T(8,128)S(1)}, f32[16,16,256]{2,1,0:T(8,128)S(1)}, u32[]{:S(2)}, u32[]{:S(2)}) collective-permute-start(f32[16,16,256]{2,1,0:T(8,128)S(1)} %fusion.43), channel_id=1, source_target_pairs={{0,256},{256,0},{1,257},{257,1},{2,258},{258,2},{3,259},{259,3},{4... | collective-permute-start | bytes 786440 | tf_op jit(solution)/shard_map/ppermute | solution.py:119
  197.6 0.2 copy.15
  197.8 0.9 broadcast_in_dim_reshape.3
  198.7 19.8 %collective-permute-done.13 = f32[16,16,256]{2,1,0:T(8,128)S(1)} collective-permute-done((f32[16,16,256]{2,1,0:T(8,128)S(1)}, f32[16,16,256]{2,1,0:T(8,128)S(1)}, u32[]{:S(2)}, u32[]{:S(2)}) %collective-permute-start.13) | collective-permute-done | bytes 262176 | tf_op jit(solution)/shard_map/ppermute | solution.py:119
  218.5 0.7 add.139
  (47 shorter events, 0.2 us)
Async XLA Ops:
  7.2 177.4 %copy-start = (bf16[2,7,128,128]{3,2,1,0:T(8,128)(2,1)S(1)}, bf16[2,7,128,128]{3,2,1,0:T(8,128)(2,1)}, u32[]{:S(2)}) copy-start(bf16[2,7,128,128]{3,2,1,0:T(8,128)(2,1)} %param.18) | copy-start | bytes 1376260
  7.2 17.0 %copy-start.2 = (f32[16,16,256]{2,1,0:T(8,128)S(1)}, f32[16,16,256]{2,1,0:T(8,128)}, u32[]{:S(2)}) copy-start(f32[16,16,256]{2,1,0:T(8,128)} %param.12) | copy-start | bytes 786436
  7.2 16.7 %copy-start.18 = (s32[16,16,256]{2,1,0:T(8,128)S(1)}, s32[16,16,256]{2,1,0:T(8,128)}, u32[]{:S(2)}) copy-start(s32[16,16,256]{2,1,0:T(8,128)} %param.14) | copy-start | bytes 786436
  7.2 17.0 %copy-start.21 = (f32[2,2,8]{2,1,0:T(2,128)S(1)}, f32[2,2,8]{2,1,0:T(2,128)}, u32[]{:S(2)}) copy-start(f32[2,2,8]{2,1,0:T(2,128)} %param.16) | copy-start | bytes 388
  7.2 174.7 %all-gather.2.cloned.1.call-start = ((), (), s32[]{:S(2)}) async-start(), calls=%async_computation | async-start | bytes 2228224 | tf_op jit(solution)/shard_map/all_gather | solution.py:108
  8.3 15.9 %collective-permute-start.2 = (f32[16,1,256]{2,1,0:T(1,128)S(1)}, f32[16,1,256]{2,1,0:T(1,128)S(1)}, u32[]{:S(2)}, u32[]{:S(2)}) collective-permute-start(f32[16,1,256]{2,1,0:T(1,128)S(1)} %get-tuple-element.29), channel_id=1, source_target_pairs={{0,16},{16,32},{32,48},{48,64},{64,80},{80,96},{96,112},{112,128},... | collective-permute-start | bytes 49160 | tf_op jit(solution)/shard_map/ppermute | solution.py:15
  10.2 13.9 %collective-permute-start.3 = (f32[16,1,256]{2,1,0:T(1,128)S(1)}, f32[16,1,256]{2,1,0:T(1,128)S(1)}, u32[]{:S(2)}, u32[]{:S(2)}) collective-permute-start(f32[16,1,256]{2,1,0:T(1,128)S(1)} %get-tuple-element.30), channel_id=1, source_target_pairs={{16,0},{32,16},{48,32},{64,48},{80,64},{96,80},{112,96},{128,112},... | collective-permute-start | bytes 49160 | tf_op jit(solution)/shard_map/ppermute | solution.py:17
  15.0 20.7 %collective-permute-start = (f32[2,16,1,256]{3,2,1,0:T(1,128)S(1)}, f32[2,16,1,256]{3,2,1,0:T(1,128)S(1)}, u32[]{:S(2)}, u32[]{:S(2)}) collective-permute-start(f32[2,16,1,256]{3,2,1,0:T(1,128)S(1)} %get-tuple-element.19), channel_id=1, source_target_pairs={{16,0},{32,16},{48,32},{64,48},{80,64},{96,80},{112,96},{128,112},... | collective-permute-start | bytes 98312 | tf_op jit(solution)/shard_map/ppermute | solution.py:17
  20.1 15.5 %collective-permute-start.1 = (f32[2,16,1,256]{3,2,1,0:T(1,128)S(1)}, f32[2,16,1,256]{3,2,1,0:T(1,128)S(1)}, u32[]{:S(2)}, u32[]{:S(2)}) collective-permute-start(f32[2,16,1,256]{3,2,1,0:T(1,128)S(1)} %get-tuple-element.20), channel_id=1, source_target_pairs={{0,16},{16,32},{32,48},{48,64},{64,80},{80,96},{96,112},{112,128},... | collective-permute-start | bytes 98312 | tf_op jit(solution)/shard_map/ppermute | solution.py:15
  24.3 11.4 %copy-start.1 = (f32[2,16,16,256]{3,2,1,0:T(8,128)S(1)}, f32[2,16,16,256]{3,2,1,0:T(8,128)}, u32[]{:S(2)}) copy-start(f32[2,16,16,256]{3,2,1,0:T(8,128)} %param.10) | copy-start | bytes 1572868
  24.4 6.7 %collective-permute-start.4 = (f32[16,18,1]{2,1,0:T(8,128)S(1)}, f32[16,18,1]{2,1,0:T(8,128)S(1)}, u32[]{:S(2)}, u32[]{:S(2)}) collective-permute-start(f32[16,18,1]{2,1,0:T(8,128)S(1)} %get-tuple-element.22), channel_id=1, source_target_pairs={{0,1},{1,2},{2,3},{3,4},{4,5},{5,6},{6,7},{7,8},{8,9},{9,10},{10,1... | collective-permute-start | bytes 3464 | tf_op jit(solution)/shard_map/ppermute | solution.py:15
  25.8 9.4 %collective-permute-start.5 = (f32[16,18,1]{2,1,0:T(8,128)S(1)}, f32[16,18,1]{2,1,0:T(8,128)S(1)}, u32[]{:S(2)}, u32[]{:S(2)}) collective-permute-start(f32[16,18,1]{2,1,0:T(8,128)S(1)} %get-tuple-element.21), channel_id=1, source_target_pairs={{1,0},{2,1},{3,2},{4,3},{5,4},{6,5},{7,6},{8,7},{9,8},{10,9},{11,1... | collective-permute-start | bytes 3464 | tf_op jit(solution)/shard_map/ppermute | solution.py:17
  36.0 11.5 %collective-permute-start.6 = (f32[2,16,18,1]{3,2,1,0:T(8,128)S(1)}, f32[2,16,18,1]{3,2,1,0:T(8,128)S(1)}, u32[]{:S(2)}, u32[]{:S(2)}) collective-permute-start(f32[2,16,18,1]{3,2,1,0:T(8,128)S(1)} %get-tuple-element.14), channel_id=1, source_target_pairs={{0,1},{1,2},{2,3},{3,4},{4,5},{5,6},{6,7},{7,8},{8,9},{9,10},{10,1... | collective-permute-start | bytes 6920 | tf_op jit(solution)/shard_map/ppermute | solution.py:15
  38.9 12.7 %collective-permute-start.7 = (f32[2,16,18,1]{3,2,1,0:T(8,128)S(1)}, f32[2,16,18,1]{3,2,1,0:T(8,128)S(1)}, u32[]{:S(2)}, u32[]{:S(2)}) collective-permute-start(f32[2,16,18,1]{3,2,1,0:T(8,128)S(1)} %get-tuple-element.13), channel_id=1, source_target_pairs={{1,0},{2,1},{3,2},{4,3},{5,4},{6,5},{7,6},{8,7},{9,8},{10,9},{11,1... | collective-permute-start | bytes 6920 | tf_op jit(solution)/shard_map/ppermute | solution.py:17
  40.8 11.6 %copy-start.3 = (f32[16,16,256]{2,1,0:T(8,128)}, f32[16,16,256]{2,1,0:T(8,128)S(1)}, u32[]{:S(2)}) copy-start(f32[16,16,256]{2,1,0:T(8,128)S(1)} %get-tuple-element.24) | copy-start | bytes 786436
  40.8 11.6 %copy-start.5 = (f32[16,16,256]{2,1,0:T(8,128)}, f32[16,16,256]{2,1,0:T(8,128)S(1)}, u32[]{:S(2)}) copy-start(f32[16,16,256]{2,1,0:T(8,128)S(1)} %get-tuple-element.25) | copy-start | bytes 786436
  40.8 11.6 %copy-start.7 = (f32[16,16,256]{2,1,0:T(8,128)}, f32[16,16,256]{2,1,0:T(8,128)S(1)}, u32[]{:S(2)}) copy-start(f32[16,16,256]{2,1,0:T(8,128)S(1)} %get-tuple-element.26) | copy-start | bytes 786436
  40.8 11.6 %copy-start.9 = (f32[16,16,256]{2,1,0:T(8,128)}, f32[16,16,256]{2,1,0:T(8,128)S(1)}, u32[]{:S(2)}) copy-start(f32[16,16,256]{2,1,0:T(8,128)S(1)} %get-tuple-element.27) | copy-start | bytes 786436
  40.8 11.6 %copy-start.11 = (f32[16,16,256]{2,1,0:T(8,128)}, f32[16,16,256]{2,1,0:T(8,128)S(1)}, u32[]{:S(2)}) copy-start(f32[16,16,256]{2,1,0:T(8,128)S(1)} %get-tuple-element.28) | copy-start | bytes 786436
  54.3 4.4 %collective-permute-start.8 = (f32[2,16,1,256]{3,2,1,0:T(1,128)S(1)}, f32[2,16,1,256]{3,2,1,0:T(1,128)S(1)}, u32[]{:S(2)}, u32[]{:S(2)}) collective-permute-start(f32[2,16,1,256]{3,2,1,0:T(1,128)S(1)} %get-tuple-element.15), channel_id=1, source_target_pairs={{16,0},{32,16},{48,32},{64,48},{80,64},{96,80},{112,96},{128,112},... | collective-permute-start | bytes 98312 | tf_op jit(solution)/shard_map/ppermute | solution.py:17
  56.2 5.2 %collective-permute-start.9 = (f32[2,16,1,256]{3,2,1,0:T(1,128)S(1)}, f32[2,16,1,256]{3,2,1,0:T(1,128)S(1)}, u32[]{:S(2)}, u32[]{:S(2)}) collective-permute-start(f32[2,16,1,256]{3,2,1,0:T(1,128)S(1)} %get-tuple-element.16), channel_id=1, source_target_pairs={{0,16},{16,32},{32,48},{48,64},{64,80},{80,96},{96,112},{112,128},... | collective-permute-start | bytes 98312 | tf_op jit(solution)/shard_map/ppermute | solution.py:15
  58.7 9.9 %copy-start.13 = (bf16[2,2,16,16,256]{4,3,2,1,0:T(8,128)(2,1)S(1)}, bf16[2,2,16,16,256]{4,3,2,1,0:T(8,128)(2,1)}, u32[]{:S(2)}) copy-start(bf16[2,2,16,16,256]{4,3,2,1,0:T(8,128)(2,1)} %param.11) | copy-start | bytes 1572868
  61.8 15.0 %copy-start.15 = (f32[2,16,16,256]{3,2,1,0:T(8,128)S(1)}, f32[2,16,16,256]{3,2,1,0:T(8,128)}, u32[]{:S(2)}) copy-start(f32[2,16,16,256]{3,2,1,0:T(8,128)} %get-tuple-element.8) | copy-start | bytes 1572868
  61.8 13.8 %collective-permute-start.10 = (f32[2,16,18,1]{3,2,1,0:T(8,128)S(1)}, f32[2,16,18,1]{3,2,1,0:T(8,128)S(1)}, u32[]{:S(2)}, u32[]{:S(2)}) collective-permute-start(f32[2,16,18,1]{3,2,1,0:T(8,128)S(1)} %get-tuple-element.11), channel_id=1, source_target_pairs={{1,0},{2,1},{3,2},{4,3},{5,4},{6,5},{7,6},{8,7},{9,8},{10,9},{11,1... | collective-permute-start | bytes 6920 | tf_op jit(solution)/shard_map/ppermute | solution.py:17
  63.2 13.6 %collective-permute-start.11 = (f32[2,16,18,1]{3,2,1,0:T(8,128)S(1)}, f32[2,16,18,1]{3,2,1,0:T(8,128)S(1)}, u32[]{:S(2)}, u32[]{:S(2)}) collective-permute-start(f32[2,16,18,1]{3,2,1,0:T(8,128)S(1)} %get-tuple-element.12), channel_id=1, source_target_pairs={{0,1},{1,2},{2,3},{3,4},{4,5},{5,6},{6,7},{7,8},{8,9},{9,10},{10,1... | collective-permute-start | bytes 6920 | tf_op jit(solution)/shard_map/ppermute | solution.py:15
  78.2 23.4 %collective-permute-start.12 = (f32[16,16,256]{2,1,0:T(8,128)S(1)}, f32[16,16,256]{2,1,0:T(8,128)S(1)}, u32[]{:S(2)}, u32[]{:S(2)}) collective-permute-start(f32[16,16,256]{2,1,0:T(8,128)S(1)} %broadcast_select_fusion), channel_id=1, source_target_pairs={{0,256},{256,0},{1,257},{257,1},{2,258},{258,2},{3,259},{259,3},{4... | collective-permute-start | bytes 786440 | tf_op jit(solution)/shard_map/ppermute | solution.py:106
  102.4 1.0 copy-start.4
  102.4 1.0 copy-start.6
  102.4 1.1 copy-start.8
  102.4 1.2 copy-start.10
  102.4 1.2 copy-start.12
  102.4 1.4 copy-start.14
  181.9 2.1 copy-start.20
  184.5 1.0 copy-start.16
  184.6 1.0 copy-start.17
  184.6 1.0 copy-start.19
  185.7 32.8 %collective-permute-start.13 = (f32[16,16,256]{2,1,0:T(8,128)S(1)}, f32[16,16,256]{2,1,0:T(8,128)S(1)}, u32[]{:S(2)}, u32[]{:S(2)}) collective-permute-start(f32[16,16,256]{2,1,0:T(8,128)S(1)} %fusion.43), channel_id=1, source_target_pairs={{0,256},{256,0},{1,257},{257,1},{2,258},{258,2},{3,259},{259,3},{4... | collective-permute-start | bytes 786440 | tf_op jit(solution)/shard_map/ppermute | solution.py:119
Sparse Core Ops, SparseCore 0:
  102.5 79.4 all-gather.1
where the time goes:
time: 227 us; the launch traced here: 226 us
  waiting for transfers between devices  135 us (59%)
  starting transfers between devices  55.7 us (25%)
  between operations  14.6 us (6%)
  other arithmetic  11.9 us (5%)
  local copies, waits for them, and re-layouts  7.91 us (3%)
    all_gather x1, waiting for transfers between devices, shards(): piece = lax.all_gather(rounded, 'gy', axis=2, tiled=True)  76.5 us
    ppermute x1, waiting for transfers between devices, shards(): sensitivity = partial_sens + lax.ppermute(partial_sens, 'sec', partner)  19.8 us
    ppermute x6, starting transfers between devices, extended(): lax.ppermute(tail, axis, [(i, (i + 1) % count) for i in range(ends)])  16 us
    ppermute x6, waiting for transfers between devices, extended(): lax.ppermute(head, axis, [((i + 1) % count, i) for i in range(ends)])  14.7 us
    ppermute x6, starting transfers between devices, extended(): lax.ppermute(head, axis, [((i + 1) % count, i) for i in range(ends)])  14.7 us
    ppermute x6, waiting for transfers between devices, extended(): lax.ppermute(tail, axis, [(i, (i + 1) % count) for i in range(ends)])  13.8 us
    ppermute x1, starting transfers between devices, shards(): rounded = (mine + lax.ppermute(other, 'sec', partner)).astype(jnp.bfloat16)  13 us
    ppermute x1, starting transfers between devices, shards(): sensitivity = partial_sens + lax.ppermute(partial_sens, 'sec', partner)  11.9 us
  transfers between devices with their start and end apart: 15, of which 10 were waited for; matrix products, arithmetic and copies ran while one was open for 4% of the time, Pallas kernels for 0%

commit v1 on v0

--- a/solution.py
+++ b/solution.py
@@ -105,7 +105,12 @@
     partner = [(0, 1), (1, 0)]
     rounded = (mine + lax.ppermute(other, "sec", partner)).astype(jnp.bfloat16)
     row_blocks, per_row, block_size, _ = blocks.shape
-    piece = lax.all_gather(rounded, "gy", axis=2, tiled=True)
+    piece = jnp.concatenate(
+        lax.all_to_all(
+            jnp.stack([rounded] * lax.axis_size("gy")), axis_name="gy", split_axis=0, concat_axis=0
+        ),
+        axis=2,
+    )
     count = piece.shape[2] // block_size
     split_rows = piece.reshape(layers, rows_x, count, block_size)
     block_ids = jnp.arange(count, dtype=jnp.int32)

time: 227 us -> 181 us (0.80)
  the two profiles are of different devices: /device:TPU:32 before, /device:TPU:83 now
where the time goes in v1:
time: 181 us; the launch traced here: 180 us
  waiting for transfers between devices  83.7 us (46%)
  starting transfers between devices  69.5 us (38%)
  other arithmetic  12.5 us (7%)
  local copies, waits for them, and re-layouts  12 us (7%)
    ppermute x6, starting transfers between devices, extended(): lax.ppermute(tail, axis, [(i, (i + 1) % count) for i in range(ends)])  22.8 us
    all_to_all x1, waiting for transfers between devices, shards(): lax.all_to_all(jnp.stack([rounded] * lax.axis_size('gy')), axis_name='gy'...  22.2 us
    ppermute x1, waiting for transfers between devices, shards(): rounded = (mine + lax.ppermute(other, 'sec', partner)).astype(jnp.bfloat16)  22.2 us
    ppermute x1, waiting for transfers between devices, shards(): sensitivity = partial_sens + lax.ppermute(partial_sens, 'sec', partner)  16.2 us
    ppermute x6, starting transfers between devices, extended(): lax.ppermute(head, axis, [((i + 1) % count, i) for i in range(ends)])  13.8 us
    ppermute x6, waiting for transfers between devices, extended(): lax.ppermute(head, axis, [((i + 1) % count, i) for i in range(ends)])  12.7 us
    ppermute x1, starting transfers between devices, shards(): rounded = (mine + lax.ppermute(other, 'sec', partner)).astype(jnp.bfloat16)  12.2 us
    ppermute x1, starting transfers between devices, shards(): sensitivity = partial_sens + lax.ppermute(partial_sens, 'sec', partner)  11 us
  transfers between devices with their start and end apart: 15, of which 10 were waited for; matrix products, arithmetic and copies ran while one was open for 6% of the time, Pallas kernels for 0%

profile of v1, /device:TPU:83, one launch (start us, length us, event | category | flops | bytes accessed | tf_op | source)
XLA Modules:
  0.0 179.8 jit_solution(7508692110517991540)
XLA Ops:
  0.6 0.0 copy-start
  0.7 1.1 fusion.57
  1.7 4.1 %collective-permute-start.2 = (f32[16,1,256]{2,1,0:T(1,128)S(1)}, f32[16,1,256]{2,1,0:T(1,128)S(1)}, u32[]{:S(2)}, u32[]{:S(2)}) collective-permute-start(f32[16,1,256]{2,1,0:T(1,128)S(1)} %get-tuple-element.29), channel_id=1, source_target_pairs={{0,16},{16,32},{32,48},{48,64},{64,80},{80,96},{96,112},{112,128},... | collective-permute-start | bytes 49160 | tf_op jit(solution)/shard_map/ppermute | solution.py:15
  5.9 1.9 %collective-permute-start.3 = (f32[16,1,256]{2,1,0:T(1,128)S(1)}, f32[16,1,256]{2,1,0:T(1,128)S(1)}, u32[]{:S(2)}, u32[]{:S(2)}) collective-permute-start(f32[16,1,256]{2,1,0:T(1,128)S(1)} %get-tuple-element.30), channel_id=1, source_target_pairs={{16,0},{32,16},{48,32},{64,48},{80,64},{96,80},{112,96},{128,112},... | collective-permute-start | bytes 49160 | tf_op jit(solution)/shard_map/ppermute | solution.py:17
  7.8 1.1 fusion.55
  8.9 2.1 %collective-permute-start = (f32[2,16,1,256]{3,2,1,0:T(1,128)S(1)}, f32[2,16,1,256]{3,2,1,0:T(1,128)S(1)}, u32[]{:S(2)}, u32[]{:S(2)}) collective-permute-start(f32[2,16,1,256]{3,2,1,0:T(1,128)S(1)} %get-tuple-element.19), channel_id=1, source_target_pairs={{16,0},{32,16},{48,32},{64,48},{80,64},{96,80},{112,96},{128,112},... | collective-permute-start | bytes 98312 | tf_op jit(solution)/shard_map/ppermute | solution.py:17
  11.0 3.4 %collective-permute-start.1 = (f32[2,16,1,256]{3,2,1,0:T(1,128)S(1)}, f32[2,16,1,256]{3,2,1,0:T(1,128)S(1)}, u32[]{:S(2)}, u32[]{:S(2)}) collective-permute-start(f32[2,16,1,256]{3,2,1,0:T(1,128)S(1)} %get-tuple-element.20), channel_id=1, source_target_pairs={{0,16},{16,32},{32,48},{48,64},{64,80},{80,96},{96,112},{112,128},... | collective-permute-start | bytes 98312 | tf_op jit(solution)/shard_map/ppermute | solution.py:15
  14.5 0.7 slice_bitcast_fusion.3
  15.2 1.1 multiply_bitcast_fusion.1
  16.3 0.1 iota_compare_fusion.4
  16.4 0.1 broadcast_and_fusion
  16.5 0.1 broadcast_compare_fusion
  16.6 0.1 pad_maximum_fusion.18
  16.7 0.1 fusion.56
  16.8 3.0 %collective-permute-start.4 = (f32[16,18,1]{2,1,0:T(8,128)S(1)}, f32[16,18,1]{2,1,0:T(8,128)S(1)}, u32[]{:S(2)}, u32[]{:S(2)}) collective-permute-start(f32[16,18,1]{2,1,0:T(8,128)S(1)} %get-tuple-element.22), channel_id=1, source_target_pairs={{0,1},{1,2},{2,3},{3,4},{4,5},{5,6},{6,7},{7,8},{8,9},{9,10},{10,1... | collective-permute-start | bytes 3464 | tf_op jit(solution)/shard_map/ppermute | solution.py:15
  19.8 2.4 %collective-permute-start.5 = (f32[16,18,1]{2,1,0:T(8,128)S(1)}, f32[16,18,1]{2,1,0:T(8,128)S(1)}, u32[]{:S(2)}, u32[]{:S(2)}) collective-permute-start(f32[16,18,1]{2,1,0:T(8,128)S(1)} %get-tuple-element.21), channel_id=1, source_target_pairs={{1,0},{2,1},{3,2},{4,3},{5,4},{6,5},{7,6},{8,7},{9,8},{10,9},{11,1... | collective-permute-start | bytes 3464 | tf_op jit(solution)/shard_map/ppermute | solution.py:17
  22.2 0.8 select_reduce_fusion
  23.1 2.1 %collective-permute-done.4 = f32[16,18,1]{2,1,0:T(8,128)S(1)} collective-permute-done((f32[16,18,1]{2,1,0:T(8,128)S(1)}, f32[16,18,1]{2,1,0:T(8,128)S(1)}, u32[]{:S(2)}, u32[]{:S(2)}) %collective-permute-start.4) | collective-permute-done | bytes 1184 | tf_op jit(solution)/shard_map/ppermute | solution.py:15
  25.2 2.9 %collective-permute-done.5 = f32[16,18,1]{2,1,0:T(8,128)S(1)} collective-permute-done((f32[16,18,1]{2,1,0:T(8,128)S(1)}, f32[16,18,1]{2,1,0:T(8,128)S(1)}, u32[]{:S(2)}, u32[]{:S(2)}) %collective-permute-start.5) | collective-permute-done | bytes 1184 | tf_op jit(solution)/shard_map/ppermute | solution.py:17
  28.1 0.4 select_maximum_fusion.8
  28.5 0.1 pad_maximum_fusion
  28.6 0.2 fusion.53
  28.8 4.9 %collective-permute-start.6 = (f32[2,16,18,1]{3,2,1,0:T(8,128)S(1)}, f32[2,16,18,1]{3,2,1,0:T(8,128)S(1)}, u32[]{:S(2)}, u32[]{:S(2)}) collective-permute-start(f32[2,16,18,1]{3,2,1,0:T(8,128)S(1)} %get-tuple-element.14), channel_id=1, source_target_pairs={{0,1},{1,2},{2,3},{3,4},{4,5},{5,6},{6,7},{7,8},{8,9},{9,10},{10,1... | collective-permute-start | bytes 6920 | tf_op jit(solution)/shard_map/ppermute | solution.py:15
  33.7 1.9 %collective-permute-start.7 = (f32[2,16,18,1]{3,2,1,0:T(8,128)S(1)}, f32[2,16,18,1]{3,2,1,0:T(8,128)S(1)}, u32[]{:S(2)}, u32[]{:S(2)}) collective-permute-start(f32[2,16,18,1]{3,2,1,0:T(8,128)S(1)} %get-tuple-element.13), channel_id=1, source_target_pairs={{1,0},{2,1},{3,2},{4,3},{5,4},{6,5},{7,6},{8,7},{9,8},{10,9},{11,1... | collective-permute-start | bytes 6920 | tf_op jit(solution)/shard_map/ppermute | solution.py:17
  35.6 0.6 fusion.41
  36.2 0.0 copy-start.7
  36.3 5.5 %collective-permute-done.6 = f32[2,16,18,1]{3,2,1,0:T(8,128)S(1)} collective-permute-done((f32[2,16,18,1]{3,2,1,0:T(8,128)S(1)}, f32[2,16,18,1]{3,2,1,0:T(8,128)S(1)}, u32[]{:S(2)}, u32[]{:S(2)}) %collective-permute-start.6) | collective-permute-done | bytes 2336 | tf_op jit(solution)/shard_map/ppermute | solution.py:15
  41.8 3.8 %collective-permute-done.7 = f32[2,16,18,1]{3,2,1,0:T(8,128)S(1)} collective-permute-done((f32[2,16,18,1]{3,2,1,0:T(8,128)S(1)}, f32[2,16,18,1]{3,2,1,0:T(8,128)S(1)}, u32[]{:S(2)}, u32[]{:S(2)}) %collective-permute-start.7) | collective-permute-done | bytes 2336 | tf_op jit(solution)/shard_map/ppermute | solution.py:17
  45.6 0.7 select_maximum_fusion.4
  46.4 1.8 %add_multiply_fusion = (f32[2,16,16,256]{3,2,1,0:T(8,128)S(1)}, f32[2,16,16,256]{3,2,1,0:T(8,128)}) fusion(f32[2,16,16,256]{3,2,1,0:T(8,128)S(1)} %select_reduce_fusion, f32[2,16,16,256]{3,2,1,0:T(8,128)S(1)} %copy-done.1, f32[2,16,1,256]{3,2,1,0:T(1,128)S(1)} %collective-permute-done.1, f32[2,16,1,256]{3,2,1,0:T(1,128)S(1)} %collective-permute-done, ...), kind=kLoop, calls=%fused_computation.87 | loop fusion | flops 4456448 | bytes 5575168 | tf_op jit(solution)/shard_map/mul | solution.py:54
  48.2 3.5 %collective-permute-start.8 = (f32[2,16,1,256]{3,2,1,0:T(1,128)S(1)}, f32[2,16,1,256]{3,2,1,0:T(1,128)S(1)}, u32[]{:S(2)}, u32[]{:S(2)}) collective-permute-start(f32[2,16,1,256]{3,2,1,0:T(1,128)S(1)} %get-tuple-element.15), channel_id=1, source_target_pairs={{16,0},{32,16},{48,32},{64,48},{80,64},{96,80},{112,96},{128,112},... | collective-permute-start | bytes 98312 | tf_op jit(solution)/shard_map/ppermute | solution.py:17
  51.7 3.8 %collective-permute-start.9 = (f32[2,16,1,256]{3,2,1,0:T(1,128)S(1)}, f32[2,16,1,256]{3,2,1,0:T(1,128)S(1)}, u32[]{:S(2)}, u32[]{:S(2)}) collective-permute-start(f32[2,16,1,256]{3,2,1,0:T(1,128)S(1)} %get-tuple-element.16), channel_id=1, source_target_pairs={{0,16},{16,32},{32,48},{48,64},{64,80},{80,96},{96,112},{112,128},... | collective-permute-start | bytes 98312 | tf_op jit(solution)/shard_map/ppermute | solution.py:15
  55.5 1.0 collective-permute-done.9
  56.5 0.1 pad_maximum_fusion.1
  56.6 0.2 fusion.52
  56.8 2.1 %collective-permute-start.10 = (f32[2,16,18,1]{3,2,1,0:T(8,128)S(1)}, f32[2,16,18,1]{3,2,1,0:T(8,128)S(1)}, u32[]{:S(2)}, u32[]{:S(2)}) collective-permute-start(f32[2,16,18,1]{3,2,1,0:T(8,128)S(1)} %get-tuple-element.11), channel_id=1, source_target_pairs={{1,0},{2,1},{3,2},{4,3},{5,4},{6,5},{7,6},{8,7},{9,8},{10,9},{11,1... | collective-permute-start | bytes 6920 | tf_op jit(solution)/shard_map/ppermute | solution.py:17
  58.8 3.5 %collective-permute-start.11 = (f32[2,16,18,1]{3,2,1,0:T(8,128)S(1)}, f32[2,16,18,1]{3,2,1,0:T(8,128)S(1)}, u32[]{:S(2)}, u32[]{:S(2)}) collective-permute-start(f32[2,16,18,1]{3,2,1,0:T(8,128)S(1)} %get-tuple-element.12), channel_id=1, source_target_pairs={{0,1},{1,2},{2,3},{3,4},{4,5},{5,6},{6,7},{7,8},{8,9},{9,10},{10,1... | collective-permute-start | bytes 6920 | tf_op jit(solution)/shard_map/ppermute | solution.py:15
  62.4 0.6 fusion.4
  63.0 6.0 %collective-permute-done.10 = f32[2,16,18,1]{3,2,1,0:T(8,128)S(1)} collective-permute-done((f32[2,16,18,1]{3,2,1,0:T(8,128)S(1)}, f32[2,16,18,1]{3,2,1,0:T(8,128)S(1)}, u32[]{:S(2)}, u32[]{:S(2)}) %collective-permute-start.10) | collective-permute-done | bytes 2336 | tf_op jit(solution)/shard_map/ppermute | solution.py:17
  68.9 1.7 collective-permute-done.11
  70.7 1.3 fusion.7
  72.0 0.1 broadcast_select_fusion
  72.1 12.2 %collective-permute-start.12 = (f32[16,16,256]{2,1,0:T(8,128)S(1)}, f32[16,16,256]{2,1,0:T(8,128)S(1)}, u32[]{:S(2)}, u32[]{:S(2)}) collective-permute-start(f32[16,16,256]{2,1,0:T(8,128)S(1)} %broadcast_select_fusion), channel_id=1, source_target_pairs={{0,256},{256,0},{1,257},{257,1},{2,258},{258,2},{3,259},{259,3},{4... | collective-permute-start | bytes 786440 | tf_op jit(solution)/shard_map/ppermute | solution.py:106
  84.3 22.2 %collective-permute-done.12 = f32[16,16,256]{2,1,0:T(8,128)S(1)} collective-permute-done((f32[16,16,256]{2,1,0:T(8,128)S(1)}, f32[16,16,256]{2,1,0:T(8,128)S(1)}, u32[]{:S(2)}, u32[]{:S(2)}) %collective-permute-start.12) | collective-permute-done | bytes 262176 | tf_op jit(solution)/shard_map/ppermute | solution.py:106
  106.5 0.1 add_convert_fusion
  106.7 1.6 stack.2
  108.2 9.7 %all-to-all-start = ((bf16[16,16,16,256]{3,2,1,0:T(8,128)(2,1)}), bf16[16,16,16,256]{3,2,1,0:T(8,128)(2,1)S(1)}, u32[]{:S(2)}, u32[]{:S(2)}) async-start(bf16[16,16,16,256]{3,2,1,0:T(8,128)(2,1)} %stack.2), calls=%async_computation | async-start | bytes 4194304 | tf_op jit(solution)/shard_map/all_to_all | solution.py:109
  117.9 0.0 copy-start.8
  118.0 1.9 %select_maximum_fusion = f32[2,18,18,258]{3,2,1,0:T(8,128)S(1)} fusion(f32[2,16,18,1]{3,2,1,0:T(8,128)S(1)} %collective-permute-done.10, f32[2,16,18,1]{3,2,1,0:T(8,128)} %copy-done.2, f32[2,16,1,256]{3,2,1,0:T(1,128)S(1)} %collective-permute-done.8, f32[2,16,16,256]{3,2,1,0:T(8,128)S(1)} %get-tuple-element.7, f32[2,16,1,256]{3,2,1,0:T(1,128)S(1)} %collective-permute-done.9), kind=kLoop, calls=%fused_computation.4 | loop fusion | flops 2006208 | bytes 1263168 | tf_op jit(solution)/shard_map/concatenate | solution.py:13
  119.9 1.7 fusion.9
  121.6 22.2 %all-to-all-done = bf16[16,16,16,256]{3,2,1,0:T(8,128)(2,1)S(1)} async-done(((bf16[16,16,16,256]{3,2,1,0:T(8,128)(2,1)}), bf16[16,16,16,256]{3,2,1,0:T(8,128)(2,1)S(1)}, u32[]{:S(2)}, u32[]{:S(2)}) %all-to-all-start) | async-done | bytes 2097184 | tf_op jit(solution)/shard_map/all_to_all | solution.py:109
  143.9 2.5 %copy.18 = bf16[16,16,16,256]{3,2,1,0:T(8,128)(2,1)} copy(bf16[16,16,16,256]{3,1,0,2:T(8,128)(2,1)S(1)} %bitcast.50) | data formatting | bytes 4194304 | tf_op jit(solution)/shard_map/reshape | solution.py:108
  146.4 2.7 %reshape.73 = bf16[16,16,32,128,1]{3,2,1,0,4:T(8,128)(2,1)S(1)} reshape(bf16[16,16,16,256]{3,2,1,0:T(8,128)(2,1)} %copy.18) | data formatting | bytes 4194304 | tf_op jit(solution)/shard_map/reshape;reshape | solution.py:115
  149.1 0.5 convolution_convert_fusion
  149.6 0.4 fusion.1
  150.1 0.5 copy-done.20
  150.6 0.1 copy-done.21
  150.6 0.0 copy-done.23
  150.7 0.1 fusion.43
  150.8 11.0 %collective-permute-start.13 = (f32[16,16,256]{2,1,0:T(8,128)S(1)}, f32[16,16,256]{2,1,0:T(8,128)S(1)}, u32[]{:S(2)}, u32[]{:S(2)}) collective-permute-start(f32[16,16,256]{2,1,0:T(8,128)S(1)} %fusion.43), channel_id=1, source_target_pairs={{0,256},{256,0},{1,257},{257,1},{2,258},{258,2},{3,259},{259,3},{4... | collective-permute-start | bytes 786440 | tf_op jit(solution)/shard_map/ppermute | solution.py:124
  161.7 0.2 copy.20
  162.0 0.9 broadcast_in_dim_reshape.3
  162.9 16.2 %collective-permute-done.13 = f32[16,16,256]{2,1,0:T(8,128)S(1)} collective-permute-done((f32[16,16,256]{2,1,0:T(8,128)S(1)}, f32[16,16,256]{2,1,0:T(8,128)S(1)}, u32[]{:S(2)}, u32[]{:S(2)}) %collective-permute-start.13) | collective-permute-done | bytes 262176 | tf_op jit(solution)/shard_map/ppermute | solution.py:124
  179.1 0.7 add.139
  (56 shorter events, 0.2 us)
Async XLA Ops:
  0.6 149.0 %copy-start = (bf16[2,7,128,128]{3,2,1,0:T(8,128)(2,1)S(1)}, bf16[2,7,128,128]{3,2,1,0:T(8,128)(2,1)}, u32[]{:S(2)}) copy-start(bf16[2,7,128,128]{3,2,1,0:T(8,128)(2,1)} %param.18) | copy-start | bytes 1376260
  0.6 15.9 %copy-start.4 = (f32[16,16,256]{2,1,0:T(8,128)S(1)}, f32[16,16,256]{2,1,0:T(8,128)}, u32[]{:S(2)}) copy-start(f32[16,16,256]{2,1,0:T(8,128)} %param.12) | copy-start | bytes 786436
  0.7 15.6 %copy-start.22 = (s32[16,16,256]{2,1,0:T(8,128)S(1)}, s32[16,16,256]{2,1,0:T(8,128)}, u32[]{:S(2)}) copy-start(s32[16,16,256]{2,1,0:T(8,128)} %param.14) | copy-start | bytes 786436
  0.7 15.9 %copy-start.25 = (f32[2,2,8]{2,1,0:T(2,128)S(1)}, f32[2,2,8]{2,1,0:T(2,128)}, u32[]{:S(2)}) copy-start(f32[2,2,8]{2,1,0:T(2,128)} %param.16) | copy-start | bytes 388
  1.7 14.8 %collective-permute-start.2 = (f32[16,1,256]{2,1,0:T(1,128)S(1)}, f32[16,1,256]{2,1,0:T(1,128)S(1)}, u32[]{:S(2)}, u32[]{:S(2)}) collective-permute-start(f32[16,1,256]{2,1,0:T(1,128)S(1)} %get-tuple-element.29), channel_id=1, source_target_pairs={{0,16},{16,32},{32,48},{48,64},{64,80},{80,96},{96,112},{112,128},... | collective-permute-start | bytes 49160 | tf_op jit(solution)/shard_map/ppermute | solution.py:15
  5.9 10.7 %collective-permute-start.3 = (f32[16,1,256]{2,1,0:T(1,128)S(1)}, f32[16,1,256]{2,1,0:T(1,128)S(1)}, u32[]{:S(2)}, u32[]{:S(2)}) collective-permute-start(f32[16,1,256]{2,1,0:T(1,128)S(1)} %get-tuple-element.30), channel_id=1, source_target_pairs={{16,0},{32,16},{48,32},{64,48},{80,64},{96,80},{112,96},{128,112},... | collective-permute-start | bytes 49160 | tf_op jit(solution)/shard_map/ppermute | solution.py:17
  8.9 19.6 %collective-permute-start = (f32[2,16,1,256]{3,2,1,0:T(1,128)S(1)}, f32[2,16,1,256]{3,2,1,0:T(1,128)S(1)}, u32[]{:S(2)}, u32[]{:S(2)}) collective-permute-start(f32[2,16,1,256]{3,2,1,0:T(1,128)S(1)} %get-tuple-element.19), channel_id=1, source_target_pairs={{16,0},{32,16},{48,32},{64,48},{80,64},{96,80},{112,96},{128,112},... | collective-permute-start | bytes 98312 | tf_op jit(solution)/shard_map/ppermute | solution.py:17
  11.0 17.5 %collective-permute-start.1 = (f32[2,16,1,256]{3,2,1,0:T(1,128)S(1)}, f32[2,16,1,256]{3,2,1,0:T(1,128)S(1)}, u32[]{:S(2)}, u32[]{:S(2)}) collective-permute-start(f32[2,16,1,256]{3,2,1,0:T(1,128)S(1)} %get-tuple-element.20), channel_id=1, source_target_pairs={{0,16},{16,32},{32,48},{48,64},{64,80},{80,96},{96,112},{112,128},... | collective-permute-start | bytes 98312 | tf_op jit(solution)/shard_map/ppermute | solution.py:15
  16.7 11.8 %copy-start.1 = (f32[2,16,16,256]{3,2,1,0:T(8,128)S(1)}, f32[2,16,16,256]{3,2,1,0:T(8,128)}, u32[]{:S(2)}) copy-start(f32[2,16,16,256]{3,2,1,0:T(8,128)} %param.10) | copy-start | bytes 1572868
  16.8 8.4 %collective-permute-start.4 = (f32[16,18,1]{2,1,0:T(8,128)S(1)}, f32[16,18,1]{2,1,0:T(8,128)S(1)}, u32[]{:S(2)}, u32[]{:S(2)}) collective-permute-start(f32[16,18,1]{2,1,0:T(8,128)S(1)} %get-tuple-element.22), channel_id=1, source_target_pairs={{0,1},{1,2},{2,3},{3,4},{4,5},{5,6},{6,7},{7,8},{8,9},{9,10},{10,1... | collective-permute-start | bytes 3464 | tf_op jit(solution)/shard_map/ppermute | solution.py:15
  19.8 8.2 %collective-permute-start.5 = (f32[16,18,1]{2,1,0:T(8,128)S(1)}, f32[16,18,1]{2,1,0:T(8,128)S(1)}, u32[]{:S(2)}, u32[]{:S(2)}) collective-permute-start(f32[16,18,1]{2,1,0:T(8,128)S(1)} %get-tuple-element.21), channel_id=1, source_target_pairs={{1,0},{2,1},{3,2},{4,3},{5,4},{6,5},{7,6},{8,7},{9,8},{10,9},{11,1... | collective-permute-start | bytes 3464 | tf_op jit(solution)/shard_map/ppermute | solution.py:17
  28.8 13.0 %collective-permute-start.6 = (f32[2,16,18,1]{3,2,1,0:T(8,128)S(1)}, f32[2,16,18,1]{3,2,1,0:T(8,128)S(1)}, u32[]{:S(2)}, u32[]{:S(2)}) collective-permute-start(f32[2,16,18,1]{3,2,1,0:T(8,128)S(1)} %get-tuple-element.14), channel_id=1, source_target_pairs={{0,1},{1,2},{2,3},{3,4},{4,5},{5,6},{6,7},{7,8},{8,9},{9,10},{10,1... | collective-permute-start | bytes 6920 | tf_op jit(solution)/shard_map/ppermute | solution.py:15
  33.7 11.9 %collective-permute-start.7 = (f32[2,16,18,1]{3,2,1,0:T(8,128)S(1)}, f32[2,16,18,1]{3,2,1,0:T(8,128)S(1)}, u32[]{:S(2)}, u32[]{:S(2)}) collective-permute-start(f32[2,16,18,1]{3,2,1,0:T(8,128)S(1)} %get-tuple-element.13), channel_id=1, source_target_pairs={{1,0},{2,1},{3,2},{4,3},{5,4},{6,5},{7,6},{8,7},{9,8},{10,9},{11,1... | collective-permute-start | bytes 6920 | tf_op jit(solution)/shard_map/ppermute | solution.py:17
  36.2 10.1 %copy-start.5 = (f32[16,16,256]{2,1,0:T(8,128)}, f32[16,16,256]{2,1,0:T(8,128)S(1)}, u32[]{:S(2)}) copy-start(f32[16,16,256]{2,1,0:T(8,128)S(1)} %get-tuple-element.23) | copy-start | bytes 786436
  36.2 10.1 %copy-start.7 = (f32[16,16,256]{2,1,0:T(8,128)}, f32[16,16,256]{2,1,0:T(8,128)S(1)}, u32[]{:S(2)}) copy-start(f32[16,16,256]{2,1,0:T(8,128)S(1)} %get-tuple-element.24) | copy-start | bytes 786436
  36.2 10.1 %copy-start.9 = (f32[16,16,256]{2,1,0:T(8,128)}, f32[16,16,256]{2,1,0:T(8,128)S(1)}, u32[]{:S(2)}) copy-start(f32[16,16,256]{2,1,0:T(8,128)S(1)} %get-tuple-element.25) | copy-start | bytes 786436
  36.2 10.1 %copy-start.11 = (f32[16,16,256]{2,1,0:T(8,128)}, f32[16,16,256]{2,1,0:T(8,128)S(1)}, u32[]{:S(2)}) copy-start(f32[16,16,256]{2,1,0:T(8,128)S(1)} %get-tuple-element.26) | copy-start | bytes 786436
  36.2 10.1 %copy-start.13 = (f32[16,16,256]{2,1,0:T(8,128)}, f32[16,16,256]{2,1,0:T(8,128)S(1)}, u32[]{:S(2)}) copy-start(f32[16,16,256]{2,1,0:T(8,128)S(1)} %get-tuple-element.27) | copy-start | bytes 786436
  36.2 10.1 %copy-start.15 = (f32[16,16,256]{2,1,0:T(8,128)}, f32[16,16,256]{2,1,0:T(8,128)S(1)}, u32[]{:S(2)}) copy-start(f32[16,16,256]{2,1,0:T(8,128)S(1)} %get-tuple-element.28) | copy-start | bytes 786436
  48.2 7.3 %collective-permute-start.8 = (f32[2,16,1,256]{3,2,1,0:T(1,128)S(1)}, f32[2,16,1,256]{3,2,1,0:T(1,128)S(1)}, u32[]{:S(2)}, u32[]{:S(2)}) collective-permute-start(f32[2,16,1,256]{3,2,1,0:T(1,128)S(1)} %get-tuple-element.15), channel_id=1, source_target_pairs={{16,0},{32,16},{48,32},{64,48},{80,64},{96,80},{112,96},{128,112},... | collective-permute-start | bytes 98312 | tf_op jit(solution)/shard_map/ppermute | solution.py:17
  51.7 4.8 %collective-permute-start.9 = (f32[2,16,1,256]{3,2,1,0:T(1,128)S(1)}, f32[2,16,1,256]{3,2,1,0:T(1,128)S(1)}, u32[]{:S(2)}, u32[]{:S(2)}) collective-permute-start(f32[2,16,1,256]{3,2,1,0:T(1,128)S(1)} %get-tuple-element.16), channel_id=1, source_target_pairs={{0,16},{16,32},{32,48},{48,64},{64,80},{80,96},{96,112},{112,128},... | collective-permute-start | bytes 98312 | tf_op jit(solution)/shard_map/ppermute | solution.py:15
  55.5 6.9 %copy-start.17 = (bf16[2,2,16,16,256]{4,3,2,1,0:T(8,128)(2,1)S(1)}, bf16[2,2,16,16,256]{4,3,2,1,0:T(8,128)(2,1)}, u32[]{:S(2)}) copy-start(bf16[2,2,16,16,256]{4,3,2,1,0:T(8,128)(2,1)} %param.11) | copy-start | bytes 1572868
  56.8 13.9 %copy-start.19 = (f32[2,16,16,256]{3,2,1,0:T(8,128)S(1)}, f32[2,16,16,256]{3,2,1,0:T(8,128)}, u32[]{:S(2)}) copy-start(f32[2,16,16,256]{3,2,1,0:T(8,128)} %get-tuple-element.8) | copy-start | bytes 1572868
  56.8 12.2 %collective-permute-start.10 = (f32[2,16,18,1]{3,2,1,0:T(8,128)S(1)}, f32[2,16,18,1]{3,2,1,0:T(8,128)S(1)}, u32[]{:S(2)}, u32[]{:S(2)}) collective-permute-start(f32[2,16,18,1]{3,2,1,0:T(8,128)S(1)} %get-tuple-element.11), channel_id=1, source_target_pairs={{1,0},{2,1},{3,2},{4,3},{5,4},{6,5},{7,6},{8,7},{9,8},{10,9},{11,1... | collective-permute-start | bytes 6920 | tf_op jit(solution)/shard_map/ppermute | solution.py:17
  58.8 11.8 %collective-permute-start.11 = (f32[2,16,18,1]{3,2,1,0:T(8,128)S(1)}, f32[2,16,18,1]{3,2,1,0:T(8,128)S(1)}, u32[]{:S(2)}, u32[]{:S(2)}) collective-permute-start(f32[2,16,18,1]{3,2,1,0:T(8,128)S(1)} %get-tuple-element.12), channel_id=1, source_target_pairs={{0,1},{1,2},{2,3},{3,4},{4,5},{5,6},{6,7},{7,8},{8,9},{9,10},{10,1... | collective-permute-start | bytes 6920 | tf_op jit(solution)/shard_map/ppermute | solution.py:15
  70.6 37.6 %copy-start.2 = (f32[2,16,18,1]{3,2,1,0:T(8,128)}, f32[2,16,18,1]{3,2,1,0:T(8,128)S(1)}, u32[]{:S(2)}) copy-start(f32[2,16,18,1]{3,2,1,0:T(8,128)S(1)} %collective-permute-done.11) | copy-start | bytes 6916
  72.1 34.5 %collective-permute-start.12 = (f32[16,16,256]{2,1,0:T(8,128)S(1)}, f32[16,16,256]{2,1,0:T(8,128)S(1)}, u32[]{:S(2)}, u32[]{:S(2)}) collective-permute-start(f32[16,16,256]{2,1,0:T(8,128)S(1)} %broadcast_select_fusion), channel_id=1, source_target_pairs={{0,256},{256,0},{1,257},{257,1},{2,258},{258,2},{3,259},{259,3},{4... | collective-permute-start | bytes 786440 | tf_op jit(solution)/shard_map/ppermute | solution.py:106
  108.2 35.6 %all-to-all-start = ((bf16[16,16,16,256]{3,2,1,0:T(8,128)(2,1)}), bf16[16,16,16,256]{3,2,1,0:T(8,128)(2,1)S(1)}, u32[]{:S(2)}, u32[]{:S(2)}) async-start(bf16[16,16,16,256]{3,2,1,0:T(8,128)(2,1)} %stack.2), calls=%async_computation | async-start | bytes 4194304 | tf_op jit(solution)/shard_map/all_to_all | solution.py:109
  117.9 2.0 %copy-start.3 = (f32[2,16,18,1]{3,2,1,0:T(8,128)S(1)}, f32[2,16,18,1]{3,2,1,0:T(8,128)}, u32[]{:S(2)}) copy-start(f32[2,16,18,1]{3,2,1,0:T(8,128)} %copy-done.2) | copy-start | bytes 6916
  117.9 2.0 %copy-start.6 = (f32[16,16,256]{2,1,0:T(8,128)S(1)}, f32[16,16,256]{2,1,0:T(8,128)}, u32[]{:S(2)}) copy-start(f32[16,16,256]{2,1,0:T(8,128)} %copy-done.5) | copy-start | bytes 786436
  117.9 2.0 %copy-start.8 = (f32[16,16,256]{2,1,0:T(8,128)S(1)}, f32[16,16,256]{2,1,0:T(8,128)}, u32[]{:S(2)}) copy-start(f32[16,16,256]{2,1,0:T(8,128)} %copy-done.7) | copy-start | bytes 786436
  117.9 2.0 %copy-start.10 = (f32[16,16,256]{2,1,0:T(8,128)S(1)}, f32[16,16,256]{2,1,0:T(8,128)}, u32[]{:S(2)}) copy-start(f32[16,16,256]{2,1,0:T(8,128)} %copy-done.9) | copy-start | bytes 786436
  117.9 2.0 %copy-start.12 = (f32[16,16,256]{2,1,0:T(8,128)S(1)}, f32[16,16,256]{2,1,0:T(8,128)}, u32[]{:S(2)}) copy-start(f32[16,16,256]{2,1,0:T(8,128)} %copy-done.11) | copy-start | bytes 786436
  118.0 2.0 %copy-start.14 = (f32[16,16,256]{2,1,0:T(8,128)S(1)}, f32[16,16,256]{2,1,0:T(8,128)}, u32[]{:S(2)}) copy-start(f32[16,16,256]{2,1,0:T(8,128)} %copy-done.13) | copy-start | bytes 786436
  118.0 2.0 %copy-start.16 = (f32[16,16,256]{2,1,0:T(8,128)S(1)}, f32[16,16,256]{2,1,0:T(8,128)}, u32[]{:S(2)}) copy-start(f32[16,16,256]{2,1,0:T(8,128)} %copy-done.15) | copy-start | bytes 786436
  118.0 2.0 %copy-start.18 = (bf16[2,2,16,16,256]{4,3,2,1,0:T(8,128)(2,1)S(1)}, bf16[2,2,16,16,256]{4,3,2,1,0:T(8,128)(2,1)}, u32[]{:S(2)}) copy-start(bf16[2,2,16,16,256]{4,3,2,1,0:T(8,128)(2,1)} %param.11) | copy-start | bytes 1572868
  146.4 2.7 %copy-start.24 = (s32[2,7]{1,0:T(2,128)S(1)}, s32[2,7]{1,0:T(2,128)}, u32[]{:S(2)}) copy-start(s32[2,7]{1,0:T(2,128)} %param.19) | copy-start | bytes 172
  149.6 1.0 copy-start.20
  149.6 1.0 copy-start.21
  149.6 1.0 copy-start.23
  150.8 28.4 %collective-permute-start.13 = (f32[16,16,256]{2,1,0:T(8,128)S(1)}, f32[16,16,256]{2,1,0:T(8,128)S(1)}, u32[]{:S(2)}, u32[]{:S(2)}) collective-permute-start(f32[16,16,256]{2,1,0:T(8,128)S(1)} %fusion.43), channel_id=1, source_target_pairs={{0,256},{256,0},{1,257},{257,1},{2,258},{258,2},{3,259},{259,3},{4... | collective-permute-start | bytes 786440 | tf_op jit(solution)/shard_map/ppermute | solution.py:124
